TPU v7x, 32 devices: a whole 2x2x4 slice. The times are simulated.
32 devices in a mesh: groups: 2 (over y), space: 4 (over x, core), chan: 4 (over z).
Axes of the slice: x: 2, y: 2, z: 4, core: 2. Of those that a mesh axis runs over, the one named last changes fastest.
Arguments:
- fields: bfloat16 [1024, 16, 256], P('chan', ('groups', 'space')), parts along dimension 1, may hold values from -6 to 6
- conv_weight: bfloat16 [27, 1024, 1024], P(None, 'chan', 'space'), may hold values from -0.0390625 to 0.0390625
Outputs:
- convolved: bfloat16 [1024, 16, 256], P('chan', ('groups', 'space')), parts along dimension 1
There are 2 independent parts, one for each index of `groups`. A program takes and returns all parts, laid end to end along the dimension named above; an argument that names none is the same for every part. Nothing has to cross between parts.
All inputs are finite; a program needn't handle non-finite values.
Results may differ from a plain program's by a relative error of at most 0.001.
Values may be sent and summed in bfloat16 or wider, within the bound.
A program may use at most 128 MiB of HBM per device.

v0:
```python
import jax
import jax.numpy as jnp
from jax import lax
from jax.sharding import PartitionSpec as P

NY = 16
NZ = 16


def padded_2(block, sides, width):
    for axis, dim in sides:
        count = lax.axis_size(axis)
        forward = [(i, i + 1) for i in range(count - 1)]
        backward = [(target, source) for source, target in forward]
        low = lax.ppermute(
            lax.slice_in_dim(block, block.shape[dim] - width, None, axis=dim), axis, forward
        )
        high = lax.ppermute(lax.slice_in_dim(block, 0, width, axis=dim), axis, backward)
        block = jnp.concatenate([low, block, high], axis=dim)
    return block


def convolve_block(summed, block, weights):
    count = block.shape[0]
    depth = block.shape[1] - 2
    shaped = block.reshape(count, depth + 2, NY, NZ)
    padded = jnp.pad(shaped, ((0, 0), (0, 0), (1, 1), (1, 1)))
    for step_x in range(3):
        for step_y in range(3):
            for step_z in range(3):
                window = padded[
                    :, step_x : step_x + depth, step_y : step_y + NY, step_z : step_z + NZ
                ].reshape(count, depth * NY * NZ)
                summed = summed + jnp.dot(
                    weights[9 * step_x + 3 * step_y + step_z],
                    window,
                    preferred_element_type=jnp.float32,
                )
    return summed


def local(fields, conv_weight):
    depth = fields.shape[1]
    owned = conv_weight.shape[1]
    weights = lax.all_gather(conv_weight, "space", axis=2, tiled=True)
    empty = jnp.zeros((owned, depth * NY * NZ), jnp.float32)
    gathered = lax.all_gather(fields, "chan", axis=0, tiled=True)
    framed = padded_2(gathered, (("space", 1),), 1)
    summed = convolve_block(empty, framed, weights)
    return summed.reshape(owned, depth, NY * NZ).astype(jnp.bfloat16)


def solution(mesh):
    return jax.shard_map(
        local,
        mesh=mesh,
        in_specs=(P("chan", ("groups", "space"), None), P(None, "chan", "space")),
        out_specs=P("chan", ("groups", "space"), None),
        check_vma=False,
    )
```

profile of v0, /device:TPU:0, one launch (start us, length us, event | category | flops | bytes accessed | tf_op | source)
XLA Modules:
  0.0 168.2 jit_solution(9444668171630820183)
XLA Ops:
  6.5 0.0 all-gather.3.cloned.1.call-start
  6.5 1.8 %copy.4 = bf16[256,2,256]{0,2,1:T(8,128)(2,1)} copy(bf16[256,2,256]{2,1,0:T(2,128)(2,1)} %param.2) | data formatting | bytes 524288 | tf_op args[0]
  8.3 0.0 all-gather.3.cloned.1.call-update
  8.4 0.0 all-gather.5.cloned.1.call-start
  8.4 0.7 all-gather.5.cloned.1.call-update
  9.1 32.5 %all-gather.3.cloned.1.call-done = bf16[1024,2,256]{0,2,1:T(8,128)(2,1)} async-done(((bf16[256,2,256]{0,2,1:T(8,128)(2,1)}), bf16[1024,2,256]{0,2,1:T(8,128)(2,1)}) %all-gather.3.cloned.1.call-update) | async-done | bytes 1048592 | tf_op jit(solution)/shard_map/all_gather | solution.py:47
  41.6 1.3 fusion.13
  42.9 1.3 collective-permute-start.1
  44.1 3.1 %collective-permute-start = (bf16[1024,1,256]{0,2,1:T(8,128)(2,1)S(1)}, bf16[1024,1,256]{0,2,1:T(8,128)(2,1)S(1)}, u32[]{:S(2)}, u32[]{:S(2)}) collective-permute-start(bf16[1024,1,256]{0,2,1:T(8,128)(2,1)S(1)} %get-tuple-element.32), channel_id=1, source_target_pairs={{0,4},{4,8},{8,12},{1,5},{5,9},{9,13},{2,6},{6,10},{10,14},{3,7},{... | collective-permute-start | bytes 1572872 | tf_op jit(solution)/shard_map/ppermute | solution.py:15
  47.2 0.0 collective-permute-done.1
  47.2 1.5 collective-permute-done
  48.7 1.6 pad_maximum_fusion
  50.3 3.4 %pad_slice_fusion.1 = (bf16[1024,2,16,16]{0,3,2,1:T(8,128)(2,1)S(1)}, bf16[1024,2,16,16]{0,3,2,1:T(8,128)(2,1)}, bf16[1024,2,16,16]{0,3,2,1:T(8,128)(2,1)S(1)}, ...) fusion(bf16[1024,4,16,16]{0,3,2,1:T(8,128)(2,1)S(1)} %bitcast.181), kind=kLoop, calls=%fused_computation.1 | loop fusion | bytes 13631488 | tf_op jit(solution)/shard_map/slice | solution.py:31
  53.7 7.4 %pad_slice_fusion = (bf16[1024,2,16,16]{0,3,2,1:T(8,128)(2,1)}, bf16[1024,2,16,16]{0,3,2,1:T(8,128)(2,1)}, bf16[1024,2,16,16]{0,3,2,1:T(8,128)(2,1)}, bf16[1024,...) fusion(bf16[1024,4,16,16]{0,3,2,1:T(8,128)(2,1)S(1)} %bitcast.182), kind=kLoop, calls=%fused_computation | loop fusion | bytes 22020096 | tf_op jit(solution)/shard_map/slice | solution.py:31
  61.1 73.3 %all-gather.5.cloned.1.call-done = bf16[27,256,1024]{2,1,0:T(8,128)(2,1)} async-done(((bf16[27,256,256]{2,1,0:T(8,128)(2,1)}), bf16[27,256,1024]{2,1,0:T(8,128)(2,1)}) %all-gather.5.cloned.1.call-update) | async-done | bytes 14155792 | tf_op jit(solution)/shard_map/all_gather | solution.py:45
  134.4 2.0 %convolution_bitcast_fusion.8 = f32[256,512]{0,1:T(8,128)S(1)} fusion(bf16[1024,512]{0,1:T(8,128)(2,1)} %bitcast.210, bf16[27,256,1024]{2,1,0:T(8,128)(2,1)} %all-gather.5.cloned.1.call-done), kind=kOutput, calls=%fused_computation.59 | convolution fusion | flops 268435456 | bytes 2097152 | tf_op jit(solution)/shard_map/dot_general | solution.py:34
  136.4 0.0 copy-start.12
  136.4 2.6 %convolution_bitcast_fusion.9 = f32[256,512]{0,1:T(8,128)S(1)} fusion(bf16[1024,512]{0,1:T(8,128)(2,1)} %bitcast.209, bf16[27,256,1024]{2,1,0:T(8,128)(2,1)} %all-gather.5.cloned.1.call-done), kind=kOutput, calls=%fused_computation.60 | convolution fusion | flops 268435456 | bytes 2097152 | tf_op jit(solution)/shard_map/dot_general | solution.py:34
  139.0 0.0 copy-start.11
  139.0 2.6 %fusion.12 = f32[512,256]{1,0:T(8,128)S(1)} fusion(bf16[1024,512]{0,1:T(8,128)(2,1)} %bitcast.208, bf16[27,256,1024]{2,1,0:T(8,128)(2,1)} %all-gather.5.cloned.1.call-done), kind=kOutput, calls=%fused_computation.89 | convolution fusion | flops 268435456 | bytes 2097152 | tf_op jit(solution)/shard_map/dot_general | solution.py:34
  141.6 0.0 copy-start.10
  141.6 1.9 %convolution_add_fusion.15 = f32[512,256]{1,0:T(8,128)S(1)} fusion(f32[512,256]{1,0:T(8,128)S(1)} %fusion.12, bf16[1024,512]{0,1:T(8,128)(2,1)} %bitcast.190, bf16[27,256,1024]{2,1,0:T(8,128)(2,1)} %all-gather.5.cloned.1.call-done), kind=kOutput, calls=%fused_computation.41 | convolution fusion | flops 268566528 | bytes 2621440 | tf_op jit(solution)/shard_map/dot_general | solution.py:34
  143.6 0.0 copy-start.3
  143.6 1.9 %convolution_add_fusion.14 = f32[512,256]{1,0:T(8,128)S(1)} fusion(f32[512,256]{1,0:T(8,128)S(1)} %convolution_add_fusion.15, bf16[1024,512]{0,1:T(8,128)(2,1)} %bitcast.206, bf16[27,256,1024]{2,1,0:T(8,128)(2,1)} %all-gather.5.cloned.1.call-done), kind=kOutput, calls=%fused_computation.40 | convolution fusion | flops 268566528 | bytes 2621440 | tf_op jit(solution)/shard_map/dot_general | solution.py:34
  145.5 0.0 copy-start.9
  145.5 1.9 %convolution_add_fusion.13 = f32[512,256]{1,0:T(8,128)S(1)} fusion(f32[512,256]{1,0:T(8,128)S(1)} %convolution_add_fusion.14, bf16[1024,512]{0,1:T(8,128)(2,1)} %bitcast.205, bf16[27,256,1024]{2,1,0:T(8,128)(2,1)} %all-gather.5.cloned.1.call-done), kind=kOutput, calls=%fused_computation.39 | convolution fusion | flops 268566528 | bytes 2621440 | tf_op jit(solution)/shard_map/dot_general | solution.py:34
  147.5 0.0 copy-done
  147.5 0.0 copy-start.8
  147.5 1.8 %convolution_add_fusion.12 = f32[512,256]{1,0:T(8,128)S(1)} fusion(f32[512,256]{1,0:T(8,128)S(1)} %convolution_add_fusion.13, bf16[1024,512]{0,1:T(8,128)(2,1)} %bitcast.189, bf16[27,256,1024]{2,1,0:T(8,128)(2,1)S(1)} %copy-done), kind=kOutput, calls=%fused_computation.38 | convolution fusion | flops 268566528 | bytes 2621440 | tf_op jit(solution)/shard_map/dot_general | solution.py:34
  149.3 0.0 copy-start.4
  149.3 1.8 %convolution_add_fusion.11 = f32[512,256]{1,0:T(8,128)S(1)} fusion(f32[512,256]{1,0:T(8,128)S(1)} %convolution_add_fusion.12, bf16[1024,512]{0,1:T(8,128)(2,1)} %bitcast.204, bf16[27,256,1024]{2,1,0:T(8,128)(2,1)S(1)} %copy-done), kind=kOutput, calls=%fused_computation.37 | convolution fusion | flops 268566528 | bytes 2621440 | tf_op jit(solution)/shard_map/dot_general | solution.py:34
  151.1 0.0 copy-done.16
  151.1 0.5 convolution_add_fusion.10
  151.6 0.0 copy-start.7
  151.6 0.0 copy-done.15
  151.6 0.5 convolution_add_fusion.9
  152.1 0.0 copy-start.6
  152.1 0.0 copy-done.14
  152.1 0.5 convolution_add_fusion.8
  152.6 0.0 copy-start.2
  152.6 0.0 copy-done.13
  152.6 0.5 convolution_add_fusion.7
  153.1 0.0 copy-start.1
  153.1 0.0 copy-done.12
  153.1 0.5 convolution_add_fusion.6
  153.6 0.0 copy-done.11
  153.6 0.5 convolution_add_fusion.5
  154.1 0.0 copy-done.10
  154.1 0.5 convolution_add_fusion.4
  154.6 0.5 convolution_add_fusion.3
  155.1 0.5 convolution_add_fusion.2
  155.6 0.5 convolution_add_fusion.1
  156.1 0.5 fusion.10
  156.6 0.5 fusion.9
  157.1 0.0 copy-done.6
  157.1 0.5 fusion.8
  157.6 0.5 fusion.7
  158.0 0.0 copy-done.1
  158.1 0.5 fusion.6
  158.5 0.5 fusion.5
  159.0 0.5 fusion.4
  159.5 0.5 fusion.3
  160.0 0.5 fusion.11
  160.5 0.9 copy.5
  (13 shorter events, 0.0 us)
Async XLA Ops:
  6.5 35.0 %all-gather.3.cloned.1.call-start = ((), (), s32[]{:S(2)}) async-start(), calls=%async_computation | async-start | bytes 1310720 | tf_op jit(solution)/shard_map/all_gather | solution.py:47
  8.4 126.0 %all-gather.5.cloned.1.call-start = ((), (), s32[]{:S(2)}) async-start(), calls=%async_computation.1 | async-start | bytes 17694720 | tf_op jit(solution)/shard_map/all_gather | solution.py:45
  42.9 4.4 %collective-permute-start.1 = (bf16[1024,1,256]{0,2,1:T(8,128)(2,1)S(1)}, bf16[1024,1,256]{0,2,1:T(8,128)(2,1)S(1)}, u32[]{:S(2)}, u32[]{:S(2)}) collective-permute-start(bf16[1024,1,256]{0,2,1:T(8,128)(2,1)S(1)} %get-tuple-element.33), channel_id=1, source_target_pairs={{4,0},{8,4},{12,8},{5,1},{9,5},{13,9},{6,2},{10,6},{14,10},{7,3},{... | collective-permute-start | bytes 1572872 | tf_op jit(solution)/shard_map/ppermute | solution.py:18
  44.1 4.6 %collective-permute-start = (bf16[1024,1,256]{0,2,1:T(8,128)(2,1)S(1)}, bf16[1024,1,256]{0,2,1:T(8,128)(2,1)S(1)}, u32[]{:S(2)}, u32[]{:S(2)}) collective-permute-start(bf16[1024,1,256]{0,2,1:T(8,128)(2,1)S(1)} %get-tuple-element.32), channel_id=1, source_target_pairs={{0,4},{4,8},{8,12},{1,5},{5,9},{9,13},{2,6},{6,10},{10,14},{3,7},{... | collective-permute-start | bytes 1572872 | tf_op jit(solution)/shard_map/ppermute | solution.py:15
  134.4 13.1 %copy-start = (bf16[27,256,1024]{2,1,0:T(8,128)(2,1)S(1)}, bf16[27,256,1024]{2,1,0:T(8,128)(2,1)}, u32[]{:S(2)}) copy-start(bf16[27,256,1024]{2,1,0:T(8,128)(2,1)} %all-gather.5.cloned.1.call-done) | copy-start | bytes 42467332
  134.4 16.7 %copy-start.16 = (bf16[1024,2,16,16]{0,3,2,1:T(8,128)(2,1)S(1)}, bf16[1024,2,16,16]{0,3,2,1:T(8,128)(2,1)}, u32[]{:S(2)}) copy-start(bf16[1024,2,16,16]{0,3,2,1:T(8,128)(2,1)} %get-tuple-element.10) | copy-start | bytes 3145732
  134.4 17.2 %copy-start.15 = (bf16[1024,2,16,16]{0,3,2,1:T(8,128)(2,1)S(1)}, bf16[1024,2,16,16]{0,3,2,1:T(8,128)(2,1)}, u32[]{:S(2)}) copy-start(bf16[1024,2,16,16]{0,3,2,1:T(8,128)(2,1)} %get-tuple-element.11) | copy-start | bytes 3145732
  134.4 17.7 %copy-start.14 = (bf16[1024,2,16,16]{0,3,2,1:T(8,128)(2,1)S(1)}, bf16[1024,2,16,16]{0,3,2,1:T(8,128)(2,1)}, u32[]{:S(2)}) copy-start(bf16[1024,2,16,16]{0,3,2,1:T(8,128)(2,1)} %get-tuple-element.12) | copy-start | bytes 3145732
  134.4 18.2 %copy-start.13 = (bf16[1024,2,16,16]{0,3,2,1:T(8,128)(2,1)S(1)}, bf16[1024,2,16,16]{0,3,2,1:T(8,128)(2,1)}, u32[]{:S(2)}) copy-start(bf16[1024,2,16,16]{0,3,2,1:T(8,128)(2,1)} %get-tuple-element.13) | copy-start | bytes 3145732
  136.4 16.7 %copy-start.12 = (bf16[1024,2,16,16]{0,3,2,1:T(8,128)(2,1)S(1)}, bf16[1024,2,16,16]{0,3,2,1:T(8,128)(2,1)}, u32[]{:S(2)}) copy-start(bf16[1024,2,16,16]{0,3,2,1:T(8,128)(2,1)} %get-tuple-element.14) | copy-start | bytes 3145732
  139.0 14.6 %copy-start.11 = (bf16[1024,2,16,16]{0,3,2,1:T(8,128)(2,1)S(1)}, bf16[1024,2,16,16]{0,3,2,1:T(8,128)(2,1)}, u32[]{:S(2)}) copy-start(bf16[1024,2,16,16]{0,3,2,1:T(8,128)(2,1)} %get-tuple-element.15) | copy-start | bytes 3145732
  141.6 12.4 %copy-start.10 = (bf16[1024,2,16,16]{0,3,2,1:T(8,128)(2,1)S(1)}, bf16[1024,2,16,16]{0,3,2,1:T(8,128)(2,1)}, u32[]{:S(2)}) copy-start(bf16[1024,2,16,16]{0,3,2,1:T(8,128)(2,1)} %get-tuple-element.16) | copy-start | bytes 3145732
  143.6 11.0 %copy-start.3 = (bf16[1024,2,16,16]{0,3,2,1:T(8,128)(2,1)S(1)}, bf16[1024,2,16,16]{0,3,2,1:T(8,128)(2,1)}, u32[]{:S(2)}) copy-start(bf16[1024,2,16,16]{0,3,2,1:T(8,128)(2,1)} %get-tuple-element.29) | copy-start | bytes 3145732
  145.5 9.6 %copy-start.9 = (bf16[1024,2,16,16]{0,3,2,1:T(8,128)(2,1)S(1)}, bf16[1024,2,16,16]{0,3,2,1:T(8,128)(2,1)}, u32[]{:S(2)}) copy-start(bf16[1024,2,16,16]{0,3,2,1:T(8,128)(2,1)} %get-tuple-element.17) | copy-start | bytes 3145732
  147.5 8.1 %copy-start.8 = (bf16[1024,2,16,16]{0,3,2,1:T(8,128)(2,1)S(1)}, bf16[1024,2,16,16]{0,3,2,1:T(8,128)(2,1)}, u32[]{:S(2)}) copy-start(bf16[1024,2,16,16]{0,3,2,1:T(8,128)(2,1)} %get-tuple-element.18) | copy-start | bytes 3145732
  149.3 6.8 %copy-start.4 = (bf16[1024,2,16,16]{0,3,2,1:T(8,128)(2,1)S(1)}, bf16[1024,2,16,16]{0,3,2,1:T(8,128)(2,1)}, u32[]{:S(2)}) copy-start(bf16[1024,2,16,16]{0,3,2,1:T(8,128)(2,1)} %get-tuple-element.19) | copy-start | bytes 3145732
  151.6 5.0 %copy-start.7 = (bf16[1024,2,16,16]{0,3,2,1:T(8,128)(2,1)S(1)}, bf16[1024,2,16,16]{0,3,2,1:T(8,128)(2,1)}, u32[]{:S(2)}) copy-start(bf16[1024,2,16,16]{0,3,2,1:T(8,128)(2,1)} %get-tuple-element.22) | copy-start | bytes 3145732
  152.1 5.0 %copy-start.6 = (bf16[1024,2,16,16]{0,3,2,1:T(8,128)(2,1)S(1)}, bf16[1024,2,16,16]{0,3,2,1:T(8,128)(2,1)}, u32[]{:S(2)}) copy-start(bf16[1024,2,16,16]{0,3,2,1:T(8,128)(2,1)} %get-tuple-element.23) | copy-start | bytes 3145732
  152.6 5.0 %copy-start.2 = (bf16[1024,2,16,16]{0,3,2,1:T(8,128)(2,1)S(1)}, bf16[1024,2,16,16]{0,3,2,1:T(8,128)(2,1)}, u32[]{:S(2)}) copy-start(bf16[1024,2,16,16]{0,3,2,1:T(8,128)(2,1)} %get-tuple-element.25) | copy-start | bytes 3145732
  153.1 5.0 %copy-start.1 = (bf16[1024,2,16,16]{0,3,2,1:T(8,128)(2,1)S(1)}, bf16[1024,2,16,16]{0,3,2,1:T(8,128)(2,1)}, u32[]{:S(2)}) copy-start(bf16[1024,2,16,16]{0,3,2,1:T(8,128)(2,1)} %get-tuple-element.28) | copy-start | bytes 3145732
  155.1 4.9 %copy-start.5 = (bf16[1024,2,16,16]{0,3,2,1:T(8,128)(2,1)S(1)}, bf16[1024,2,16,16]{0,3,2,1:T(8,128)(2,1)}, u32[]{:S(2)}) copy-start(bf16[1024,2,16,16]{0,3,2,1:T(8,128)(2,1)} %get-tuple-element.5) | copy-start | bytes 3145732
Sparse Core Ops, SparseCore 0:
  8.9 32.6 all-gather.2
  43.1 91.1 all-gather.4
where the time goes:
time: 169 us; the launch traced here: 168 us
  waiting for transfers between devices  108 us (64%)
  matrix products  25.6 us (15%)
  local copies, waits for them, and re-layouts  14.8 us (9%)
  between operations  13.9 us (8%)
  starting transfers between devices  4.4 us (3%)
    all_gather x1, waiting for transfers between devices, local(): weights = lax.all_gather(conv_weight, 'space', axis=2, tiled=True)  73.3 us
    all_gather x1, waiting for transfers between devices, local(): gathered = lax.all_gather(fields, 'chan', axis=0, tiled=True)  32.5 us
    dot_general x27, matrix products, convolve_block(): jnp.dot(weights[9 * step_x + 3 * step_y + step_z], window, preferred_elem...  25.6 us
    slice x2, local copies, waits for them, and re-layouts, convolve_block(): padded[:, step_x:step_x + depth, step_y:step_y + NY, step_z:step_z + NZ]  10.8 us
  transfers between devices with their start and end apart: 4, of which 3 were waited for; matrix products, arithmetic and copies ran while one was open for 8% of the time, Pallas kernels for 0%

commit v1 on v0

--- a/solution.py
+++ b/solution.py
@@ -42,7 +42,8 @@
 def local(fields, conv_weight):
     depth = fields.shape[1]
     owned = conv_weight.shape[1]
-    weights = lax.all_gather(conv_weight, "space", axis=2, tiled=True)
+    parts = lax.all_gather(conv_weight, "space", axis=0, tiled=False)
+    weights = jnp.concatenate(parts, axis=2)
     empty = jnp.zeros((owned, depth * NY * NZ), jnp.float32)
     gathered = lax.all_gather(fields, "chan", axis=0, tiled=True)
     framed = padded_2(gathered, (("space", 1),), 1)

time: 169 us -> 228 us (1.35)
  local copies, waits for them, and re-layouts: 14.8 us -> 83.5 us
  matrix products: 25.6 us -> 15.2 us
    slice x0 -> x29, local copies, waits for them, and re-layouts: none -> 66.9 us  [convolve_block(): weights[9 * step_x + 3 * step_y + step_z]]
    dot_general x27, matrix products: 25.6 us -> 15.2 us  [convolve_block(): jnp.dot(weights[9 * step_x + 3 * step_y + step_z], window, preferred_elem...]
    ppermute x1, waiting for transfers between devices: 0.01 us -> 3.21 us  [padded_2(): lax.ppermute(lax.slice_in_dim(block, 0, width, axis=dim), axis, backward)]
  transfers between devices with their start and end apart: 4 -> 4, of which waited for: 3 -> 4; matrix products, arithmetic and copies ran while one was open for 8% -> 6% of each run, Pallas kernels for 0% -> 0%
where the time goes in v1:
time: 228 us; the launch traced here: 226 us
  waiting for transfers between devices  109 us (48%)
  local copies, waits for them, and re-layouts  83.5 us (37%)
  matrix products  15.2 us (7%)
  between operations  14.2 us (6%)
  starting transfers between devices  2.66 us (1%)
    all_gather x1, waiting for transfers between devices, local(): parts = lax.all_gather(conv_weight, 'space', axis=0, tiled=False)  72.3 us
    slice x29, local copies, waits for them, and re-layouts, convolve_block(): weights[9 * step_x + 3 * step_y + step_z]  66.9 us
    all_gather x1, waiting for transfers between devices, local(): gathered = lax.all_gather(fields, 'chan', axis=0, tiled=True)  32.5 us
    dot_general x27, matrix products, convolve_block(): jnp.dot(weights[9 * step_x + 3 * step_y + step_z], window, preferred_elem...  15.2 us
    slice x2, local copies, waits for them, and re-layouts, convolve_block(): padded[:, step_x:step_x + depth, step_y:step_y + NY, step_z:step_z + NZ]  11.4 us
  transfers between devices with their start and end apart: 4, of which 4 were waited for; matrix products, arithmetic and copies ran while one was open for 6% of the time, Pallas kernels for 0%

profile of v1, /device:TPU:0, one launch (start us, length us, event | category | flops | bytes accessed | tf_op | source)
XLA Modules:
  0.0 225.9 jit_solution(15484407728358232687)
XLA Ops:
  6.5 1.8 copy.35
  8.4 0.7 all-gather.6.cloned.1.call-update
  9.1 32.5 %all-gather.4.cloned.1.call-done = bf16[1024,2,256]{0,2,1:T(8,128)(2,1)} async-done(((bf16[256,2,256]{0,2,1:T(8,128)(2,1)}), bf16[1024,2,256]{0,2,1:T(8,128)(2,1)}) %all-gather.4.cloned.1.call-update) | async-done | bytes 1048592 | tf_op jit(solution)/shard_map/all_gather | solution.py:48
  41.6 1.3 fusion.14
  42.9 1.3 collective-permute-start
  44.2 1.3 collective-permute-start.1
  45.7 3.2 %collective-permute-done.1 = bf16[1024,1,256]{0,2,1:T(8,128)(2,1)S(1)} collective-permute-done((bf16[1024,1,256]{0,2,1:T(8,128)(2,1)S(1)}, bf16[1024,1,256]{0,2,1:T(8,128)(2,1)S(1)}, u32[]{:S(2)}, u32[]{:S(2)}) %collective-permute-start.1) | collective-permute-done | bytes 524320 | tf_op jit(solution)/shard_map/ppermute | solution.py:18
  48.9 1.6 pad_maximum_fusion
  50.5 3.0 %pad_slice_fusion.1 = (bf16[1024,2,16,16]{0,3,2,1:T(8,128)(2,1)S(1)}, bf16[1024,2,16,16]{0,3,2,1:T(8,128)(2,1)}, bf16[1024,2,16,16]{0,3,2,1:T(8,128)(2,1)S(1)}, ...) fusion(bf16[1024,4,16,16]{0,3,2,1:T(8,128)(2,1)S(1)} %bitcast.157), kind=kLoop, calls=%fused_computation.1 | loop fusion | bytes 13631488 | tf_op jit(solution)/shard_map/slice | solution.py:31
  53.6 8.3 %pad_slice_fusion = (bf16[1024,2,16,16]{0,3,2,1:T(8,128)(2,1)}, bf16[1024,2,16,16]{0,3,2,1:T(8,128)(2,1)}, bf16[1024,2,16,16]{0,3,2,1:T(8,128)(2,1)}, bf16[1024,...) fusion(bf16[1024,4,16,16]{0,3,2,1:T(8,128)(2,1)S(1)} %bitcast.158), kind=kLoop, calls=%fused_computation | loop fusion | bytes 22020096 | tf_op jit(solution)/shard_map/slice | solution.py:31
  61.9 72.3 %all-gather.6.cloned.1.call-done = bf16[108,256,256]{2,1,0:T(8,128)(2,1)} async-done(((bf16[27,256,256]{2,1,0:T(8,128)(2,1)}), bf16[108,256,256]{2,1,0:T(8,128)(2,1)}) %all-gather.6.cloned.1.call-update) | async-done | bytes 14155792 | tf_op jit(solution)/shard_map/all_gather | solution.py:45
  134.1 4.2 %fusion.13 = (bf16[1,256,4,256]{3,1,0,2:T(8,128)(2,1)}, bf16[1,256,4,256]{3,1,0,2:T(8,128)(2,1)}, bf16[1,256,4,256]{3,1,0,2:T(8,128)(2,1)}, bf16[1,256,4,256]{3,...) fusion(bf16[27,256,4,256]{3,1,0,2:T(8,128)(2,1)} %bitcast.159), kind=kLoop, calls=%fused_computation.64 | loop fusion | bytes 8388608 | tf_op jit(solution)/shard_map/slice | solution.py:35
  138.3 7.4 %fusion.12 = (bf16[1,256,4,256]{3,1,0,2:T(8,128)(2,1)}, bf16[1,256,4,256]{3,1,0,2:T(8,128)(2,1)}, bf16[1,256,4,256]{3,1,0,2:T(8,128)(2,1)}, bf16[1,256,4,256]{3,...) fusion(bf16[27,256,4,256]{3,1,0,2:T(8,128)(2,1)} %bitcast.160), kind=kLoop, calls=%fused_computation.63 | loop fusion | bytes 19922944 | tf_op jit(solution)/shard_map/slice | solution.py:35
  145.7 2.1 copy.62
  147.7 2.0 copy.43
  149.8 2.0 copy.42
  151.8 2.0 copy.41
  153.9 2.1 copy.40
  155.9 2.0 copy.39
  158.0 2.1 copy.38
  160.1 2.0 copy.37
  162.1 2.1 copy.36
  164.2 2.0 copy.61
  166.2 2.0 copy.60
  168.2 2.0 copy.59
  170.3 2.0 copy.58
  172.3 2.0 copy.57
  174.4 2.0 copy.56
  176.4 2.0 copy.55
  178.5 2.0 copy.54
  180.5 2.0 copy.53
  182.6 2.0 copy.52
  184.6 2.1 copy.51
  186.7 2.0 copy.50
  188.8 2.1 copy.49
  190.8 2.0 copy.48
  192.9 2.0 copy.47
  194.9 2.1 copy.46
  197.0 2.1 copy.45
  199.1 2.1 copy.44
  201.1 1.9 convolution_bitcast_fusion.8
  203.1 1.9 convolution_bitcast_fusion.9
  205.1 0.4 fusion.15
  205.5 0.4 convolution_add_fusion.15
  206.0 0.4 convolution_add_fusion.14
  206.5 0.4 convolution_add_fusion.13
  207.0 0.4 convolution_add_fusion.12
  207.6 0.4 convolution_add_fusion.11
  208.1 0.4 convolution_add_fusion.10
  209.6 0.4 convolution_add_fusion.7
  210.1 0.4 convolution_add_fusion.6
  211.2 0.4 convolution_add_fusion.4
  211.7 0.4 convolution_add_fusion.3
  212.3 0.4 convolution_add_fusion.2
  212.8 0.4 convolution_add_fusion.1
  213.3 0.4 fusion.10
  214.7 0.7 fusion.8
  215.4 0.4 fusion.7
  215.9 0.4 fusion.6
  216.4 0.5 fusion.5
  216.8 0.5 fusion.4
  217.3 0.5 fusion.3
  217.8 0.4 fusion.11
  218.2 0.9 copy.63
  (102 shorter events, 3.2 us)
Async XLA Ops:
  6.5 35.0 %all-gather.4.cloned.1.call-start = ((), (), s32[]{:S(2)}) async-start(), calls=%async_computation | async-start | bytes 1310720 | tf_op jit(solution)/shard_map/all_gather | solution.py:48
  8.4 125.8 %all-gather.6.cloned.1.call-start = ((), (), s32[]{:S(2)}) async-start(), calls=%async_computation.1 | async-start | bytes 17694720 | tf_op jit(solution)/shard_map/all_gather | solution.py:45
  42.9 2.8 %collective-permute-start = (bf16[1024,1,256]{0,2,1:T(8,128)(2,1)S(1)}, bf16[1024,1,256]{0,2,1:T(8,128)(2,1)S(1)}, u32[]{:S(2)}, u32[]{:S(2)}) collective-permute-start(bf16[1024,1,256]{0,2,1:T(8,128)(2,1)S(1)} %get-tuple-element.59), channel_id=1, source_target_pairs={{0,4},{4,8},{8,12},{1,5},{5,9},{9,13},{2,6},{6,10},{10,14},{3,7},{... | collective-permute-start | bytes 1572872 | tf_op jit(solution)/shard_map/ppermute | solution.py:15
  44.2 4.7 %collective-permute-start.1 = (bf16[1024,1,256]{0,2,1:T(8,128)(2,1)S(1)}, bf16[1024,1,256]{0,2,1:T(8,128)(2,1)S(1)}, u32[]{:S(2)}, u32[]{:S(2)}) collective-permute-start(bf16[1024,1,256]{0,2,1:T(8,128)(2,1)S(1)} %get-tuple-element.60), channel_id=1, source_target_pairs={{4,0},{8,4},{12,8},{5,1},{9,5},{13,9},{6,2},{10,6},{14,10},{7,3},{... | collective-permute-start | bytes 1572872 | tf_op jit(solution)/shard_map/ppermute | solution.py:18
  201.1 3.9 %copy-start.21 = (bf16[1024,2,16,16]{0,3,2,1:T(8,128)(2,1)S(1)}, bf16[1024,2,16,16]{0,3,2,1:T(8,128)(2,1)}, u32[]{:S(2)}) copy-start(bf16[1024,2,16,16]{0,3,2,1:T(8,128)(2,1)} %get-tuple-element.33) | copy-start | bytes 3145732
  201.1 3.9 %copy-start.46 = (bf16[1,256,4,256]{1,3,2,0:T(8,128)(2,1)S(1)}, bf16[1,256,4,256]{1,3,2,0:T(8,128)(2,1)}, u32[]{:S(2)}) copy-start(bf16[1,256,4,256]{1,3,2,0:T(8,128)(2,1)} %copy.37) | copy-start | bytes 1572868
  201.1 4.4 %copy-start.4 = (bf16[1024,2,16,16]{0,3,2,1:T(8,128)(2,1)S(1)}, bf16[1024,2,16,16]{0,3,2,1:T(8,128)(2,1)}, u32[]{:S(2)}) copy-start(bf16[1024,2,16,16]{0,3,2,1:T(8,128)(2,1)} %get-tuple-element.58) | copy-start | bytes 3145732
  201.1 4.4 %copy-start.42 = (bf16[1,256,4,256]{1,3,2,0:T(8,128)(2,1)S(1)}, bf16[1,256,4,256]{1,3,2,0:T(8,128)(2,1)}, u32[]{:S(2)}) copy-start(bf16[1,256,4,256]{1,3,2,0:T(8,128)(2,1)} %copy.36) | copy-start | bytes 1572868
  203.1 2.9 %copy-start.20 = (bf16[1024,2,16,16]{0,3,2,1:T(8,128)(2,1)S(1)}, bf16[1024,2,16,16]{0,3,2,1:T(8,128)(2,1)}, u32[]{:S(2)}) copy-start(bf16[1024,2,16,16]{0,3,2,1:T(8,128)(2,1)} %get-tuple-element.34) | copy-start | bytes 3145732
  203.1 2.9 %copy-start.40 = (bf16[1,256,4,256]{1,3,2,0:T(8,128)(2,1)S(1)}, bf16[1,256,4,256]{1,3,2,0:T(8,128)(2,1)}, u32[]{:S(2)}) copy-start(bf16[1,256,4,256]{1,3,2,0:T(8,128)(2,1)} %copy.38) | copy-start | bytes 1572868
  205.0 1.5 copy-start.19
  205.0 1.5 copy-start.38
  205.5 1.5 copy-start.3
  205.5 1.5 copy-start.36
  206.0 1.5 copy-start.18
  206.0 1.5 copy-start.34
  206.5 1.5 copy-start.17
  206.5 1.5 copy-start.32
  207.0 1.5 copy-start.16
  207.0 1.5 copy-start.30
  207.6 1.4 copy-start.15
  207.6 1.6 copy-start.44
  208.0 1.5 copy-start.14
  208.1 1.5 copy-start.43
  208.5 1.5 copy-start.13
  208.5 1.5 copy-start.41
  209.1 1.4 copy-start.12
  209.1 1.6 copy-start.39
  209.6 1.6 copy-start.11
  209.6 1.6 copy-start.37
  210.1 1.6 copy-start.2
  210.1 1.6 copy-start.35
  210.7 1.4 copy-start.10
  210.7 1.6 copy-start.33
  211.2 1.6 copy-start.9
  211.2 1.6 copy-start.31
  211.7 1.6 copy-start.5
  211.7 1.6 copy-start.29
  212.7 1.3 copy-start.8
  212.7 1.5 copy-start.28
  213.2 1.4 copy-start.7
  213.2 1.4 copy-start.27
  213.7 1.7 copy-start.1
  213.7 1.7 copy-start.26
  214.2 1.6 copy-start
  214.2 1.6 copy-start.25
  214.7 1.6 copy-start.24
  215.4 1.4 copy-start.23
  215.9 1.4 copy-start.22
  216.3 1.4 copy-start.6
  216.3 1.4 copy-start.45
Sparse Core Ops, SparseCore 0:
  8.9 32.6 all-gather.3
  43.1 90.9 all-gather.5
